TPU v7x, 32 devices: a whole 2x2x4 slice. The times are simulated.
32 devices in a mesh: dp: 16 (over z, x, core), inner: 2 (over y).
Axes of the slice: x: 2, y: 2, z: 4, core: 2. Of those that a mesh axis runs over, the one named last changes fastest.
Arguments:
- grad_parts: bfloat16 [32, 20, 256, 256], P(('dp', 'inner')), may hold values from -0.125 to 0.125
- owner: int32 [20], replicated, may hold values from 0 to 15, as said below
- weights: bfloat16 [32, 256, 256], P('dp'), may hold values from -0.375 to 0.375
- first_moment: float32 [32, 256, 256], P('dp'), may hold values from -1.5 to 1.5
- second_moment: float32 [32, 256, 256], P('dp'), may hold values from 0.01 to 0.1
- left_stats: float32 [32, 256, 256], P('dp'), may hold values from -5 to 10, as said below
- right_stats: float32 [32, 256, 256], P('dp'), may hold values from -5 to 10, as said below
- left_basis: float32 [32, 256, 256], P('dp'), may hold values from -0.375 to 0.375
- right_basis: float32 [32, 256, 256], P('dp'), may hold values from -0.375 to 0.375
Outputs:
- new_weights: bfloat16 [20, 256, 256], replicated
- first_out: float32 [32, 256, 256], P('dp')
- second_out: float32 [32, 256, 256], P('dp')
- left_stats_out: float32 [32, 256, 256], P('dp')
- right_stats_out: float32 [32, 256, 256], P('dp')
- left_basis_out: float32 [32, 256, 256], P('dp')
- right_basis_out: float32 [32, 256, 256], P('dp')
Inputs may be any that keep to these rules, and one draw needn't show every extreme that they name: owner[b] is the dp index holding block b's state; no dp index owns more than 2 blocks, and one owns exactly 2. left_stats is symmetric. right_stats is symmetric.
All inputs are finite; a program needn't handle non-finite values.
Results may differ from a plain program's by a relative error of at most 0.002.
Values may be sent and summed in bfloat16 or wider, within the bound.
A program may use at most 64 MiB of HBM per device.

v0:
```python
import jax
import jax.numpy as jnp
from jax import lax
from jax.sharding import PartitionSpec as P

NS_STEPS = 5


SMOOTHING = 0.95
BIAS_CORRECTION = 1.0 - 0.95**10
LEARNING_RATE = 0.01
PRECISE = lax.Precision.HIGHEST


def slot_targets(owner, capacity):
    count = owner.shape[0]
    index = jnp.arange(count, dtype=jnp.int32)
    earlier = (owner[:, None] == owner[None, :]) & (index[None, :] < index[:, None])
    return owner * capacity + jnp.sum(earlier.astype(jnp.int32), axis=1)


def orthonormalize(power):
    norm = jnp.sqrt(jnp.sum(power * power, axis=(1, 2), keepdims=True))
    current = power / (norm + 1e-06)
    for step in range(NS_STEPS):
        square = jnp.einsum("cij,ckj->cik", current, current, precision=PRECISE)
        current = 1.5 * current - 0.5 * jnp.einsum(
            "cik,ckj->cij", square, current, precision=PRECISE
        )
    return current


def local(
    grad_parts,
    owner,
    weights,
    first_moment,
    second_moment,
    left_stats,
    right_stats,
    left_basis,
    right_basis,
):
    dp_count = lax.axis_size("dp")
    inner_count = lax.axis_size("inner")
    capacity = weights.shape[0]
    matrix_order = weights.shape[1]
    block_count = owner.shape[0]
    row_share = matrix_order // inner_count
    row_sums = lax.psum_scatter(
        grad_parts[0].astype(jnp.float32).astype(jnp.bfloat16),
        "inner",
        scatter_dimension=1,
        tiled=True,
    ).astype(jnp.float32)
    target = slot_targets(owner, capacity)
    placing = (jnp.arange(dp_count * capacity, dtype=jnp.int32)[:, None] == target[None, :]).astype(
        jnp.float32
    )
    packed = jnp.dot(
        placing,
        row_sums.reshape(block_count, row_share * matrix_order),
        precision=PRECISE,
        preferred_element_type=jnp.float32,
    )
    owned = lax.psum_scatter(
        packed.reshape(dp_count * capacity, row_share, matrix_order).astype(jnp.bfloat16),
        "dp",
        scatter_dimension=0,
        tiled=True,
    ).astype(jnp.float32)
    grad = lax.all_gather(owned.astype(jnp.bfloat16), "inner", axis=1, tiled=True).astype(
        owned.dtype
    )
    half_turn = jnp.einsum("cik,cil->ckl", left_basis, grad, precision=PRECISE)
    rotated = jnp.einsum("ckl,clm->ckm", half_turn, right_basis, precision=PRECISE)
    first_out = SMOOTHING * first_moment + (1.0 - SMOOTHING) * rotated
    second_out = SMOOTHING * second_moment + (1.0 - SMOOTHING) * rotated * rotated
    direction = first_out / BIAS_CORRECTION / (jnp.sqrt(second_out / BIAS_CORRECTION) + 1e-08)
    back_turn = jnp.einsum("cik,ckl->cil", left_basis, direction, precision=PRECISE)
    update = jnp.einsum("cil,cml->cim", back_turn, right_basis, precision=PRECISE)
    new_rows = (weights.astype(jnp.float32) - LEARNING_RATE * update).astype(jnp.bfloat16)
    slot_number = target - owner * capacity
    mine = lax.dynamic_slice_in_dim(new_rows, lax.axis_index("inner") * row_share, row_share, 1)
    everything = lax.all_gather(mine, ("dp", "inner"), axis=1, tiled=True)
    flat = everything.reshape(capacity * dp_count, matrix_order, matrix_order)
    new_weights = jnp.take(flat, slot_number * dp_count + owner, axis=0)
    left_stats_out = SMOOTHING * left_stats + (1.0 - SMOOTHING) * jnp.einsum(
        "cil,cjl->cij", grad, grad, precision=PRECISE
    )
    right_stats_out = SMOOTHING * right_stats + (1.0 - SMOOTHING) * jnp.einsum(
        "cli,clj->cij", grad, grad, precision=PRECISE
    )
    left_power = jnp.einsum("cij,cjk->cik", left_stats_out, left_basis, precision=PRECISE)
    right_power = jnp.einsum("cij,cjk->cik", right_stats_out, right_basis, precision=PRECISE)
    left_basis_out = orthonormalize(left_power)
    right_basis_out = orthonormalize(right_power)
    return (
        new_weights,
        first_out,
        second_out,
        left_stats_out,
        right_stats_out,
        left_basis_out,
        right_basis_out,
    )


def solution(mesh):
    in_specs = (
        P(("dp", "inner"), None, None, None),
        P(),
        P("dp", None, None),
        P("dp", None, None),
        P("dp", None, None),
        P("dp", None, None),
        P("dp", None, None),
        P("dp", None, None),
        P("dp", None, None),
    )
    out_specs = (
        P(),
        P("dp", None, None),
        P("dp", None, None),
        P("dp", None, None),
        P("dp", None, None),
        P("dp", None, None),
        P("dp", None, None),
    )
    return jax.shard_map(local, mesh=mesh, in_specs=in_specs, out_specs=out_specs, check_vma=False)
```

profile of v0, /device:TPU:25, one launch (start us, length us, event | category | flops | bytes accessed | tf_op | source)
XLA Modules:
  0.0 198.0 jit_solution(13558100158738389395)
XLA Ops:
  8.2 40.7 %reduce-scatter.3.cloned.1.call-done = bf16[20,128,256]{2,1,0:T(8,128)(2,1)} async-done(((bf16[20,256,256]{2,1,0:T(8,128)(2,1)}), bf16[20,128,256]{2,1,0:T(8,128)(2,1)}) %reduce-scatter.3.cloned.1.call-update) | async-done | bytes 1310736 | tf_op jit(solution)/shard_map/reduce_scatter | solution.py:50
  48.9 1.4 slice_bitcast_fusion
  50.3 1.2 convolution_convert_fusion
  51.5 2.5 %copy.37 = bf16[32,128,256]{2,1,0:T(8,128)(2,1)} copy(bf16[32,128,256]{2,0,1:T(8,128)(2,1)S(1)} %convolution_convert_fusion) | data formatting | bytes 4194304 | tf_op jit(solution)/shard_map/convert_element_type | solution.py:67
  54.1 58.9 %reduce-scatter.5.cloned.1.call-done = bf16[2,128,256]{2,1,0:T(8,128)(2,1)} async-done(((bf16[32,128,256]{2,1,0:T(8,128)(2,1)}), bf16[2,128,256]{2,1,0:T(8,128)(2,1)}) %reduce-scatter.5.cloned.1.call-update) | async-done | bytes 131088 | tf_op jit(solution)/shard_map/reduce_scatter | solution.py:66
  113.0 1.0 copy.38
  114.0 4.7 %all_gather.6 = bf16[2,256,256]{2,0,1:T(2,128)(2,1)S(1)} all-gather(bf16[2,128,256]{2,0,1:T(2,128)(2,1)S(1)} %copy.38), channel_id=1, replica_groups=mesh['dp'=16,'inner'=2] {'inner'}, dimensions={1}, use_global_device_ids=true | all-gather | bytes 393216 | tf_op jit(solution)/shard_map/all_gather | solution.py:72
  119.6 0.8 multiply_add_fusion
  120.4 0.9 fusion.14
  122.0 0.7 fusion.21
  123.0 0.8 multiply_reduce_fusion.1
  124.1 0.8 multiply_reduce_fusion
  124.9 0.8 fusion.26
  125.6 0.8 fusion.27
  126.4 0.8 fusion.10
  127.9 0.7 fusion.9
  130.6 0.7 fusion.7
  131.9 1.7 fusion.6
  133.7 0.8 fusion.5
  136.5 0.7 fusion.3
  139.2 1.5 fusion.1
  140.7 46.1 %all-gather.2.cloned.1.call-done = bf16[2,4096,256]{2,1,0:T(8,128)(2,1)} async-done(((bf16[2,128,256]{2,1,0:T(8,128)(2,1)}), bf16[2,4096,256]{2,1,0:T(8,128)(2,1)}) %all-gather.2.cloned.1.call-update) | async-done | bytes 4194320 | tf_op jit(solution)/shard_map/all_gather | solution.py:85
  186.8 2.9 %gather_fusion = bf16[20,256,256]{2,1,0:T(8,128)(2,1)S(1)} fusion(bf16[32,256,256]{2,1,0:T(8,128)(2,1)} %bitcast.64, s32[1024]{0:T(1024)S(1)} %pad_clamp_fusion), kind=kCustom, calls=%fused_computation | custom fusion | bytes 5242960 | tf_op jit(solution)/shard_map/jit(_take)/gather | solution.py:87
  189.7 1.8 broadcast_select_fusion
  (52 shorter events, 10.5 us)
Async XLA Ops:
  7.2 112.4 %copy-start = (f32[2,256,256]{2,1,0:T(8,128)S(1)}, f32[2,256,256]{2,1,0:T(8,128)}, u32[]{:S(2)}) copy-start(f32[2,256,256]{2,1,0:T(8,128)} %param.17) | copy-start | bytes 1572868
  7.2 0.8 copy-start.11
  7.2 41.7 %reduce-scatter.3.cloned.1.call-start = ((), (), s32[]{:S(2)}) async-start(), calls=%async_computation.2 | async-start | bytes 3932160 | tf_op jit(solution)/shard_map/reduce_scatter | solution.py:50
  7.9 105.0 %reduce-scatter.5.cloned.1.call-start = ((), (), s32[]{:S(2)}) async-start(), calls=%async_computation.3 | async-start | bytes 2228224 | tf_op jit(solution)/shard_map/reduce_scatter | solution.py:66
  54.0 64.9 %copy-start.2 = (f32[2,256,256]{2,1,0:T(8,128)S(1)}, f32[2,256,256]{2,1,0:T(8,128)}, u32[]{:S(2)}) copy-start(f32[2,256,256]{2,1,0:T(8,128)} %param.16) | copy-start | bytes 1572868
  54.0 65.5 %copy-start.6 = (f32[2,256,256]{2,1,0:T(8,128)S(1)}, f32[2,256,256]{2,1,0:T(8,128)}, u32[]{:S(2)}) copy-start(f32[2,256,256]{2,1,0:T(8,128)} %param.12) | copy-start | bytes 1572868
  54.0 65.5 %copy-start.7 = (f32[2,256,256]{2,1,0:T(8,128)S(1)}, f32[2,256,256]{2,1,0:T(8,128)}, u32[]{:S(2)}) copy-start(f32[2,256,256]{2,1,0:T(8,128)} %param.13) | copy-start | bytes 1572868
  54.0 132.8 %all-gather.2.cloned.1.call-start = ((), (), s32[]{:S(2)}) async-start(), calls=%async_computation.4 | async-start | bytes 4325376 | tf_op jit(solution)/shard_map/all_gather | solution.py:85
  120.3 1.6 copy-start.8
  120.3 1.6 copy-start.9
  120.3 1.6 copy-start.10
  120.4 2.4 %copy-start.5 = (f32[2,256,256]{2,1,0:T(8,128)S(1)}, f32[2,256,256]{2,1,0:T(8,128)}, u32[]{:S(2)}) copy-start(f32[2,256,256]{2,1,0:T(8,128)} %param.14) | copy-start | bytes 1572868
  122.0 1.9 copy-start.4
  123.0 0.8 copy-start.3
  124.1 1.5 copy-start.1
Sparse Core Ops, SparseCore 0:
  10.3 38.5 reduce-scatter.2
  54.2 58.7 reduce-scatter.4
  122.8 63.9 all-gather.1
where the time goes:
time: 201 us; the launch traced here: 198 us
  waiting for transfers between devices  146 us (73%)
  matrix products  21.8 us (11%)
  between operations  14.1 us (7%)
  local copies, waits for them, and re-layouts  8.12 us (4%)
  blocking collectives  4.68 us (2%)
  other arithmetic  2.73 us (1%)
    reduce_scatter x1, waiting for transfers between devices, local(): lax.psum_scatter(packed.reshape(dp_count * capacity, row_share, matrix_or...  58.9 us
    all_gather x1, waiting for transfers between devices, local(): everything = lax.all_gather(mine, ('dp', 'inner'), axis=1, tiled=True)  46.1 us
    reduce_scatter x1, waiting for transfers between devices, local(): lax.psum_scatter(grad_parts[0].astype(jnp.float32).astype(jnp.bfloat16),...  40.7 us
    dot_general x10, matrix products, orthonormalize(): jnp.einsum('cik,ckj->cij', square, current, precision=PRECISE)  8.85 us
    dot_general x10, matrix products, orthonormalize(): square = jnp.einsum('cij,ckj->cik', current, current, precision=PRECISE)  6.79 us
    all_gather x1, blocking collectives, local(): lax.all_gather(owned.astype(jnp.bfloat16), 'inner', axis=1, tiled=True)  4.68 us
  transfers between devices with their start and end apart: 3, of which 3 were waited for; matrix products, arithmetic and copies ran while one was open for 9% of the time, Pallas kernels for 0%

commit v1 on v0

v1 whole, which is shorter than its diff:
```python
import functools

import jax
import jax.numpy as jnp
from jax import lax
from jax.experimental import pallas as pl
from jax.experimental.pallas import tpu as pltpu
from jax.sharding import PartitionSpec as P

NS_STEPS = 5


SMOOTHING = 0.95
BIAS_CORRECTION = 1.0 - 0.95**10
LEARNING_RATE = 0.01
PRECISE = lax.Precision.HIGH
MESH = pl.DeviceIdType.MESH
CORES = 2
XS = 2
PIECES = 4


def slot_numbers(owner):
    count = owner.shape[0]
    index = jnp.arange(count, dtype=jnp.int32)
    earlier = (owner[:, None] == owner[None, :]) & (index[None, :] < index[:, None])
    return jnp.sum(earlier.astype(jnp.int32), axis=1)


def position(inner_count):
    d = lax.axis_index("dp")
    c = lax.rem(d, CORES)
    x = lax.rem(d // CORES, XS)
    z = d // (CORES * XS)
    i = lax.axis_index("inner")
    return z, x, c, i


def dp_of(z, x, c):
    return (z * XS + x) * CORES + c


class Copies:
    def __init__(self, send, recv):
        self.send, self.recv, self.made = send, recv, []

    def start(self, src, dst, device):
        n = len(self.made)
        copy = pltpu.make_async_remote_copy(
            src_ref=src,
            dst_ref=dst,
            send_sem=self.send.at[n],
            recv_sem=self.recv.at[n],
            device_id=device,
            device_id_type=MESH,
        )
        copy.start()
        self.made.append(copy)
        return copy

    def finish(self):
        for copy in self.made:
            copy.wait_send()


def greet(devices):
    barrier = pltpu.get_barrier_semaphore()
    for device in devices:
        pl.semaphore_signal(barrier, inc=1, device_id=device, device_id_type=MESH)
    pl.semaphore_wait(barrier, len(devices))


def plane_offsets(inner_count):
    return [
        (dx, dc, di)
        for di in range(inner_count)
        for dx in range(XS)
        for dc in range(CORES)
        if (dx, dc, di) != (0, 0, 0)
    ]


def reduce_kernel(
    zs, inner, cap, nb, rows,
    block_ref, valid_ref, g_ref, out_ref,
    b1, s1, r2a, s2a, f2a, r3a, r2b, s2b, f2b, r3b, total, zsend, zown, zrecv, psend, gbuf,
    send, recv,
):
    z, x, c, i = position(inner)
    f32, bf16 = jnp.float32, jnp.bfloat16
    here = dp_of(z, x, c)
    core_peer = (dp_of(z, x, 1 - c), i)
    x_peer = (dp_of(z, 1 - x, c), i)

    def inner_peer(m):
        return (here, lax.rem(i + m, inner))

    def z_peer(k):
        return (dp_of(lax.rem(z + k, zs), x, c), i)

    def plane_peer(dx, dc, di):
        return (dp_of(z, lax.rem(x + dx, XS), lax.rem(c + dc, CORES)), lax.rem(i + di, inner))

    offsets = plane_offsets(inner)
    greet([plane_peer(*o) for o in offsets] + [z_peer(k) for k in range(1, zs)])

    copies = Copies(send, recv)
    half = nb // 2
    size = nb // PIECES
    pieces = []
    for p in range(PIECES // 2):
        pieces += [(True, p * size), (False, half + p * size)]

    first = [
        copies.start(g_ref.at[pl.ds(lo, size), 1 - c], b1.at[pl.ds(lo, size)], core_peer)
        for _, lo in pieces
    ]
    second = []
    for (inner_first, lo), arrived in zip(pieces, first):
        arrived.wait_recv()

        @pl.loop(lo, lo + size)
        def _(b):
            s1[b] = (g_ref[b, c].astype(f32) + b1[b].astype(f32)).astype(bf16)

        if inner_first:
            second.append([
                copies.start(
                    s1.at[pl.ds(lo, size), :, lax.rem(i + m, inner)],
                    r2a.at[m - 1, pl.ds(lo, size)],
                    inner_peer(m),
                )
                for m in range(1, inner)
            ])
        else:
            second.append([
                copies.start(
                    s1.at[pl.ds(lo, size), 1 - x], r2b.at[pl.ds(lo - half, size)], x_peer
                )
            ])
    third = []
    for (inner_first, lo), arrived in zip(pieces, second):
        for copy in arrived:
            copy.wait_recv()
        if inner_first:

            @pl.loop(lo, lo + size)
            def _(b):
                value = g_ref[b, c, :, i].astype(f32) + b1[b, :, i].astype(f32)
                for m in range(1, inner):
                    value = value + r2a[m - 1, b].astype(f32)
                f2a[b] = value
                s2a[b] = value.astype(bf16)

            third.append([
                copies.start(s2a.at[pl.ds(lo, size), 1 - x], r3a.at[pl.ds(lo, size)], x_peer)
            ])
        else:

            @pl.loop(lo, lo + size)
            def _(b):
                value = g_ref[b, c, x].astype(f32) + b1[b, x].astype(f32)
                value = value + r2b[b - half].astype(f32)
                f2b[b - half] = value
                s2b[b - half] = value.astype(bf16)

            third.append([
                copies.start(
                    s2b.at[pl.ds(lo - half, size), lax.rem(i + m, inner)],
                    r3b.at[m - 1, pl.ds(lo - half, size)],
                    inner_peer(m),
                )
                for m in range(1, inner)
            ])
    for (inner_first, lo), arrived in zip(pieces, third):
        for copy in arrived:
            copy.wait_recv()
        if inner_first:

            @pl.loop(lo, lo + size)
            def _(b):
                total[b] = f2a[b, x] + r3a[b].astype(f32)

        else:

            @pl.loop(lo, lo + size)
            def _(b):
                value = f2b[b - half, i]
                for m in range(1, inner):
                    value = value + r3b[m - 1, b - half].astype(f32)
                total[b] = value

    plane = XS * CORES * cap

    def slot_value(slot):
        value = total[block_ref[slot]]
        return jnp.where(valid_ref[slot] > 0, value, jnp.zeros_like(value))

    fourth = []
    for k in range(1, zs):
        there = lax.rem(z + k, zs)

        @pl.loop(0, plane)
        def _(s):
            zsend[k - 1, s] = slot_value(there * plane + s).astype(bf16)

        fourth.append(copies.start(zsend.at[k - 1], zrecv.at[k - 1], z_peer(k)))

    @pl.loop(0, plane)
    def _(s):
        zown[s] = slot_value(z * plane + s)

    for copy in fourth:
        copy.wait_recv()

    @pl.loop(0, plane)
    def _(s):
        value = zown[s]
        for k in range(1, zs):
            value = value + zrecv[k - 1, s].astype(f32)
        psend[s] = value.astype(bf16)

    share = (c * XS + x) * inner + i
    fifth = []
    for dx, dc, di in offsets:
        to = lax.rem(x + dx, XS) * CORES + lax.rem(c + dc, CORES)
        fifth.append(
            copies.start(
                psend.at[pl.ds(to * cap, cap)], gbuf.at[share], plane_peer(dx, dc, di)
            )
        )
    gbuf[share] = psend[pl.ds((x * CORES + c) * cap, cap)]
    for copy in fifth:
        copy.wait_recv()
    for s in range(CORES * XS * inner):
        out_ref[:, s * rows : (s + 1) * rows, :] = gbuf[s].astype(f32)
    copies.finish()


def reduce_grads(zs, inner, cap, grad_parts, block, valid):
    nb, order = grad_parts.shape[0], grad_parts.shape[1]
    rows = order // (CORES * XS * inner)
    half = nb // 2
    plane = XS * CORES * cap
    f32, bf16 = jnp.float32, jnp.bfloat16
    tile = (rows, order)
    g = grad_parts.reshape(nb, CORES, XS, inner, rows, order)
    offsets = len(plane_offsets(inner))
    count = PIECES + PIECES * inner + (zs - 1) + offsets
    smem = pl.BlockSpec(memory_space=pltpu.SMEM)
    vmem = pl.BlockSpec(memory_space=pltpu.VMEM)
    return pl.pallas_call(
        functools.partial(reduce_kernel, zs, inner, cap, nb, rows),
        out_shape=jax.ShapeDtypeStruct((cap, order, order), f32),
        in_specs=[smem, smem, vmem],
        out_specs=vmem,
        scratch_shapes=[
            pltpu.VMEM((nb, XS, inner) + tile, bf16),
            pltpu.VMEM((nb, XS, inner) + tile, bf16),
            pltpu.VMEM((inner - 1, half, XS) + tile, bf16),
            pltpu.VMEM((half, XS) + tile, bf16),
            pltpu.VMEM((half, XS) + tile, f32),
            pltpu.VMEM((half,) + tile, bf16),
            pltpu.VMEM((half, inner) + tile, bf16),
            pltpu.VMEM((half, inner) + tile, bf16),
            pltpu.VMEM((half, inner) + tile, f32),
            pltpu.VMEM((inner - 1, half) + tile, bf16),
            pltpu.VMEM((nb,) + tile, f32),
            pltpu.VMEM((zs - 1, plane) + tile, bf16),
            pltpu.VMEM((plane,) + tile, f32),
            pltpu.VMEM((zs - 1, plane) + tile, bf16),
            pltpu.VMEM((plane,) + tile, bf16),
            pltpu.VMEM((CORES * XS * inner, cap) + tile, bf16),
            pltpu.SemaphoreType.DMA((count,)),
            pltpu.SemaphoreType.DMA((count,)),
        ],
        compiler_params=pltpu.CompilerParams(collective_id=0, has_side_effects=True),
    )(block, valid, g)


def gather_kernel(zs, inner, cap, nb, rows, place_ref, mine_ref, out_ref, held, send, recv):
    z, x, c, i = position(inner)
    here = dp_of(z, x, c)
    core_peer = (dp_of(z, x, 1 - c), i)
    x_peer = (dp_of(z, 1 - x, c), i)

    def inner_peer(m):
        return (here, lax.rem(i + m, inner))

    def z_peer(k):
        return (dp_of(lax.rem(z + k, zs), x, c), i)

    greet(
        [core_peer, x_peer]
        + [inner_peer(m) for m in range(1, inner)]
        + [z_peer(k) for k in range(1, zs)]
    )
    copies = Copies(send, recv)
    own = held.at[z, x, i, c]
    along_z = [copies.start(mine_ref, own, z_peer(k)) for k in range(1, zs)]
    to_x, to_inner, to_core = [], [], []
    for k in range(zs):
        from_z = lax.rem(z + zs - k, zs)
        slot = held.at[from_z, x, i, c]
        if k > 0:
            along_z[k - 1].wait_recv()
        src = mine_ref if k == 0 else slot
        to_x.append(copies.start(src, slot, x_peer))
        to_inner.append([copies.start(src, slot, inner_peer(m)) for m in range(1, inner)])
        to_core.append(copies.start(src, slot, core_peer))
    held[z, x, i, c] = mine_ref[...]
    corner = []
    for k in range(zs):
        from_z = lax.rem(z + zs - k, zs)
        slot = held.at[from_z, 1 - x, i, c]
        to_x[k].wait_recv()
        ahead = [
            copies.start(slot.at[0], slot.at[0], inner_peer(m)) for m in range(1, inner)
        ]
        to_core.append(copies.start(slot, slot, core_peer))
        for m in range(1, inner):
            from_i = lax.rem(i + inner - m, inner)
            slot = held.at[from_z, x, from_i, c]
            to_inner[k][m - 1].wait_recv()
            across = copies.start(slot.at[1], slot.at[1], x_peer)
            to_core.append(copies.start(slot, slot, core_peer))
            corner.append((from_z, from_i, ahead[m - 1], across))
    for from_z, from_i, ahead, across in corner:
        slot = held.at[from_z, 1 - x, from_i, c]
        ahead.wait_recv()
        to_core.append(copies.start(slot.at[0], slot.at[0], core_peer))
        across.wait_recv()
        to_core.append(copies.start(slot.at[1], slot.at[1], core_peer))
    for copy in to_core:
        copy.wait_recv()

    @pl.loop(0, nb)
    def _(b):
        bz, bx, bc, bk = (place_ref[n, b] for n in range(4))
        for part in range(inner):
            for h in range(2):
                lo = (part * 2 + h) * rows
                out_ref[b, lo : lo + rows, :] = held[bz, bx, part, bc, h, bk]

    copies.finish()


def gather_weights(zs, inner, nb, new_rows, owner, slot_number):
    cap, order = new_rows.shape[0], new_rows.shape[1]
    rows = order // (inner * 2)
    mine = lax.dynamic_slice_in_dim(
        new_rows, lax.axis_index("inner") * 2 * rows, 2 * rows, 1
    )
    mine = mine.reshape(cap, 2, rows, order).swapaxes(0, 1)
    place = jnp.stack(
        [owner // (XS * CORES), (owner // CORES) % XS, owner % CORES, slot_number]
    ).astype(jnp.int32)
    others = inner - 1
    count = (zs - 1) + zs * (2 + others) + zs * (1 + 3 * others) + zs * 2 * others
    smem = pl.BlockSpec(memory_space=pltpu.SMEM)
    vmem = pl.BlockSpec(memory_space=pltpu.VMEM)
    return pl.pallas_call(
        functools.partial(gather_kernel, zs, inner, cap, nb, rows),
        out_shape=jax.ShapeDtypeStruct((nb, order, order), jnp.bfloat16),
        in_specs=[smem, vmem],
        out_specs=vmem,
        scratch_shapes=[
            pltpu.VMEM((zs, XS, inner, CORES, 2, cap, rows, order), jnp.bfloat16),
            pltpu.SemaphoreType.DMA((count,)),
            pltpu.SemaphoreType.DMA((count,)),
        ],
        compiler_params=pltpu.CompilerParams(collective_id=1, has_side_effects=True),
    )(place, mine)


def orthonormalize(power):
    norm = jnp.sqrt(jnp.sum(power * power, axis=(1, 2), keepdims=True))
    current = power / (norm + 1e-06)
    for step in range(NS_STEPS):
        square = jnp.einsum("cij,ckj->cik", current, current, precision=PRECISE)
        current = 1.5 * current - 0.5 * jnp.einsum(
            "cik,ckj->cij", square, current, precision=PRECISE
        )
    return current


def local(
    grad_parts,
    owner,
    weights,
    first_moment,
    second_moment,
    left_stats,
    right_stats,
    left_basis,
    right_basis,
):
    dp_count = lax.axis_size("dp")
    inner_count = lax.axis_size("inner")
    capacity = weights.shape[0]
    block_count = owner.shape[0]
    zs = dp_count // (XS * CORES)
    slot_number = slot_numbers(owner)
    target = owner * capacity + slot_number
    match = jnp.arange(dp_count * capacity, dtype=jnp.int32)[:, None] == target[None, :]
    valid = jnp.sum(match.astype(jnp.int32), axis=1)
    block = jnp.sum(
        jnp.where(match, jnp.arange(block_count, dtype=jnp.int32)[None, :], 0), axis=1
    )
    grad = reduce_grads(zs, inner_count, capacity, grad_parts[0], block, valid)
    half_turn = jnp.einsum("cik,cil->ckl", left_basis, grad, precision=PRECISE)
    rotated = jnp.einsum("ckl,clm->ckm", half_turn, right_basis, precision=PRECISE)
    first_out = SMOOTHING * first_moment + (1.0 - SMOOTHING) * rotated
    second_out = SMOOTHING * second_moment + (1.0 - SMOOTHING) * rotated * rotated
    direction = first_out / BIAS_CORRECTION / (jnp.sqrt(second_out / BIAS_CORRECTION) + 1e-08)
    back_turn = jnp.einsum("cik,ckl->cil", left_basis, direction, precision=PRECISE)
    update = jnp.einsum("cil,cml->cim", back_turn, right_basis, precision=PRECISE)
    new_rows = (weights.astype(jnp.float32) - LEARNING_RATE * update).astype(jnp.bfloat16)
    new_weights = gather_weights(zs, inner_count, block_count, new_rows, owner, slot_number)
    left_stats_out = SMOOTHING * left_stats + (1.0 - SMOOTHING) * jnp.einsum(
        "cil,cjl->cij", grad, grad, precision=PRECISE
    )
    right_stats_out = SMOOTHING * right_stats + (1.0 - SMOOTHING) * jnp.einsum(
        "cli,clj->cij", grad, grad, precision=PRECISE
    )
    left_power = jnp.einsum("cij,cjk->cik", left_stats_out, left_basis, precision=PRECISE)
    right_power = jnp.einsum("cij,cjk->cik", right_stats_out, right_basis, precision=PRECISE)
    left_basis_out = orthonormalize(left_power)
    right_basis_out = orthonormalize(right_power)
    return (
        new_weights,
        first_out,
        second_out,
        left_stats_out,
        right_stats_out,
        left_basis_out,
        right_basis_out,
    )


def solution(mesh):
    dp = P("dp", None, None)
    in_specs = (P(("dp", "inner"), None, None, None), P()) + (dp,) * 7
    out_specs = (P(),) + (dp,) * 6
    return jax.shard_map(local, mesh=mesh, in_specs=in_specs, out_specs=out_specs, check_vma=False)
```

time: 201 us -> 93.6 us (0.47); the launches traced: 198 us -> 93.4 us
  waiting for transfers between devices: 146 us -> 0 us
  Pallas kernels: 0 us -> 70.8 us
  between operations: 14.1 us -> 1.04 us
  matrix products: 21.8 us -> 15.6 us
  local copies, waits for them, and re-layouts: 8.12 us -> 2.99 us
  blocking collectives: 4.68 us -> 0 us
    reduce_scatter x2 -> x0, waiting for transfers between devices: 99.6 us -> none  [the longest x1 58.9 us: local(): lax.psum_scatter(packed.reshape(dp_count * capacity, row_share, matrix_or...]
    pallas_call x0 -> x2, Pallas kernels: none -> 70.8 us  [the longest x1 38.4 us: reduce_grads(): pl.pallas_call(functools.partial(reduce_kernel, zs, inner, cap, nb, rows)...]
    all_gather x1 -> x0, waiting for transfers between devices: 46.1 us -> none  [local(): everything = lax.all_gather(mine, ('dp', 'inner'), axis=1, tiled=True)]
    all_gather x1 -> x0, blocking collectives: 4.68 us -> none  [local(): lax.all_gather(owned.astype(jnp.bfloat16), 'inner', axis=1, tiled=True)]
    dot_general x10, matrix products: 8.85 us -> 5.93 us  [orthonormalize(): jnp.einsum('cik,ckj->cij', square, current, precision=PRECISE)]
    gather x1 -> x0, local copies, waits for them, and re-layouts: 2.9 us -> none  [local(): new_weights = jnp.take(flat, slot_number * dp_count + owner, axis=0)]
    convert_element_type x1 -> x0, local copies, waits for them, and re-layouts: 2.51 us -> none  [local(): packed.reshape(dp_count * capacity, row_share, matrix_order)]
    dot_general x10, matrix products: 6.79 us -> 4.39 us  [orthonormalize(): square = jnp.einsum('cij,ckj->cik', current, current, precision=PRECISE)]
  transfers between devices with their start and end apart: 3 -> 0, of which waited for: 3 -> 0; matrix products, arithmetic and copies ran while one was open for 9% -> 0% of each run, Pallas kernels for 0% -> 0%
where the time goes in v1:
time: 93.6 us; the launch traced here: 93.4 us
  Pallas kernels  70.8 us (76%)
  matrix products  15.6 us (17%)
  local copies, waits for them, and re-layouts  2.99 us (3%)
  other arithmetic  2.92 us (3%)
  between operations  1.04 us (1%)
    pallas_call x1, Pallas kernels, reduce_grads(): pl.pallas_call(functools.partial(reduce_kernel, zs, inner, cap, nb, rows)...  38.4 us
    pallas_call x1, Pallas kernels, gather_weights(): pl.pallas_call(functools.partial(gather_kernel, zs, inner, cap, nb, rows)...  32.4 us
    dot_general x10, matrix products, orthonormalize(): jnp.einsum('cik,ckj->cij', square, current, precision=PRECISE)  5.93 us
    dot_general x10, matrix products, orthonormalize(): square = jnp.einsum('cij,ckj->cik', current, current, precision=PRECISE)  4.39 us
    unnamed x27, local copies, waits for them, and re-layouts  2.32 us

profile of v1, /device:TPU:25, one launch (start us, length us, event | category | flops | bytes accessed | tf_op | source)
XLA Modules:
  0.0 93.4 jit_solution(5472753730248784519)
XLA Ops:
  0.7 1.0 %convert_reduce_fusion.1 = s32[20]{0:T(128)S(1)} fusion(s32[20]{0:T(128)} %param.10), kind=kLoop, calls=%fused_computation.48 | loop fusion | flops 1980 | bytes 160 | tf_op jit(solution)/shard_map/reduce_sum | solution.py:27
  1.7 0.7 multiply_add_fusion.1
  2.4 0.6 pad_add_fusion.place_ref
  2.9 0.6 convert_reduce_fusion
  3.5 38.4 %shard_map.144 = f32[2,256,256]{2,1,0:T(8,128)} custom-call(s32[32]{0:T(128)} %get-tuple-element.8.block_ref, s32[32]{0:T(128)} %get-tuple-element.7.valid_ref, bf16[20,2,2,2,32,256]{5,4,3,2,1,0:T(8,128)(2,1)} %bitcast.61), custom_call_target="tpu_custom_call" | custom-call | tf_op jit(solution)/shard_map/pallas_call | solution.py:252
  42.0 1.7 %fusion.32 = f32[2,256,256]{1,2,0:T(8,128)S(1)} fusion(f32[2,256,256]{2,1,0:T(8,128)} %shard_map.144, f32[2,256,256]{2,1,0:T(8,128)S(1)} %copy-done.3), kind=kOutput, calls=%fused_computation.73 | convolution fusion | flops 201326592 | bytes 1572864 | tf_op jit(solution)/shard_map/cik,cil->ckl/dot_general | solution.py:411
  43.7 0.5 multiply_add_fusion
  44.2 0.8 copy-done.11
  45.0 0.6 fusion.13
  46.2 0.7 copy.31
  46.8 32.4 %shard_map.145 = bf16[20,256,256]{2,1,0:T(8,128)(2,1)} custom-call(s32[4,20]{1,0:T(4,128)} %pad_add_fusion.place_ref, bf16[2,2,64,256]{3,2,1,0:T(8,128)(2,1)} %bitcast.63), custom_call_target="tpu_custom_call" | custom-call | tf_op jit(solution)/shard_map/pallas_call | solution.py:362
  79.3 0.5 fusion.11
  79.8 0.7 fusion.10
  80.4 0.5 multiply_reduce_fusion.1
  80.9 0.5 fusion.23
  81.5 0.5 fusion.9
  82.0 0.4 fusion.34
  82.8 0.4 fusion.35
  85.0 1.2 %fusion.5 = f32[2,256,256]{2,1,0:T(8,128)} fusion(f32[2,256,256]{2,1,0:T(8,128)S(1)} %fusion.37, f32[2,256,256]{2,1,0:T(8,128)S(1)} %fusion.6), kind=kOutput, calls=%fused_computation.11 | convolution fusion | flops 201719808 | bytes 1572864 | tf_op jit(solution)/shard_map/cik,ckj->cij/dot_general | solution.py:381
  86.2 0.5 multiply_reduce_fusion
  86.7 0.5 fusion.24
  87.2 0.5 fusion.4
  90.7 1.2 %fusion = f32[2,256,256]{2,1,0:T(8,128)} fusion(f32[2,256,256]{2,1,0:T(8,128)S(1)} %fusion.41, f32[2,256,256]{2,1,0:T(8,128)S(1)} %fusion.1), kind=kOutput, calls=%fused_computation.1 | convolution fusion | flops 201719808 | bytes 1572864 | tf_op jit(solution)/shard_map/cik,ckj->cij/dot_general | solution.py:381
  91.9 1.5 %copy.33 = bf16[20,256,256]{2,1,0:T(8,128)(2,1)} copy(bf16[20,256,256]{2,1,0:T(8,128)(2,1)S(1)} %copy-done.2) | data formatting | bytes 5242880
  (41 shorter events, 5.6 us)
Async XLA Ops:
  0.6 43.0 %copy-start = (f32[2,256,256]{2,1,0:T(8,128)S(1)}, f32[2,256,256]{2,1,0:T(8,128)}, u32[]{:S(2)}) copy-start(f32[2,256,256]{2,1,0:T(8,128)} %param.17) | copy-start | bytes 1572868
  0.6 41.3 %copy-start.3 = (f32[2,256,256]{2,1,0:T(8,128)S(1)}, f32[2,256,256]{2,1,0:T(8,128)}, u32[]{:S(2)}) copy-start(f32[2,256,256]{2,1,0:T(8,128)} %param.16) | copy-start | bytes 1572868
  0.7 43.0 %copy-start.6 = (f32[2,256,256]{2,1,0:T(8,128)S(1)}, f32[2,256,256]{2,1,0:T(8,128)}, u32[]{:S(2)}) copy-start(f32[2,256,256]{2,1,0:T(8,128)} %param.12) | copy-start | bytes 1572868
  0.7 43.0 %copy-start.7 = (f32[2,256,256]{2,1,0:T(8,128)S(1)}, f32[2,256,256]{2,1,0:T(8,128)}, u32[]{:S(2)}) copy-start(f32[2,256,256]{2,1,0:T(8,128)} %param.13) | copy-start | bytes 1572868
  44.2 0.8 copy-start.11
  44.2 35.0 %copy-start.10 = (f32[2,256,256]{2,1,0:T(8,128)}, f32[2,256,256]{2,1,0:T(8,128)S(1)}, u32[]{:S(2)}) copy-start(f32[2,256,256]{2,1,0:T(8,128)S(1)} %get-tuple-element.27) | copy-start | bytes 1572868
  44.2 1.9 %copy-start.12 = (bf16[2,256,256]{2,1,0:T(8,128)(2,1)S(1)}, bf16[2,256,256]{2,1,0:T(8,128)(2,1)}, u32[]{:S(2)}) copy-start(bf16[2,256,256]{2,1,0:T(8,128)(2,1)} %param.11) | copy-start | bytes 786436
  45.6 33.6 %copy-start.1 = (f32[2,256,256]{2,1,0:T(8,128)S(1)}, f32[2,256,256]{2,1,0:T(8,128)}, u32[]{:S(2)}) copy-start(f32[2,256,256]{2,1,0:T(8,128)} %shard_map.144) | copy-start | bytes 1572868
  45.6 33.6 %copy-start.8 = (f32[2,256,256]{2,1,0:T(8,128)S(1)}, f32[2,256,256]{2,1,0:T(8,128)}, u32[]{:S(2)}) copy-start(f32[2,256,256]{2,1,0:T(8,128)} %param.14) | copy-start | bytes 1572868
  46.1 33.6 %copy-start.9 = (f32[2,256,256]{2,1,0:T(8,128)S(1)}, f32[2,256,256]{2,1,0:T(8,128)}, u32[]{:S(2)}) copy-start(f32[2,256,256]{2,1,0:T(8,128)} %param.15) | copy-start | bytes 1572868
  79.7 1.7 %copy-start.4 = (f32[2,256,256]{2,1,0:T(8,128)}, f32[2,256,256]{2,1,0:T(8,128)S(1)}, u32[]{:S(2)}) copy-start(f32[2,256,256]{2,1,0:T(8,128)S(1)} %fusion.11) | copy-start | bytes 1572868
  80.4 5.8 %copy-start.5 = (f32[2,256,256]{2,1,0:T(8,128)}, f32[2,256,256]{2,1,0:T(8,128)S(1)}, u32[]{:S(2)}) copy-start(f32[2,256,256]{2,1,0:T(8,128)S(1)} %fusion.10) | copy-start | bytes 1572868
  89.8 2.1 %copy-start.2 = (bf16[20,256,256]{2,1,0:T(8,128)(2,1)S(1)}, bf16[20,256,256]{2,1,0:T(8,128)(2,1)}, u32[]{:S(2)}) copy-start(bf16[20,256,256]{2,1,0:T(8,128)(2,1)} %shard_map.145) | copy-start | bytes 7864324

commit v2 on v1

v2 whole, which is shorter than its diff:
```python
import functools

import jax
import jax.numpy as jnp
from jax import lax
from jax.experimental import pallas as pl
from jax.experimental.pallas import tpu as pltpu
from jax.sharding import PartitionSpec as P

NS_STEPS = 5


SMOOTHING = 0.95
BIAS_CORRECTION = 1.0 - 0.95**10
LEARNING_RATE = 0.01
MESH = pl.DeviceIdType.MESH
CORES = 2
XS = 2
PIECES = 4


def position(inner_count):
    d = lax.axis_index("dp")
    c = lax.rem(d, CORES)
    x = lax.rem(d // CORES, XS)
    z = d // (CORES * XS)
    i = lax.axis_index("inner")
    return z, x, c, i


def dp_of(z, x, c):
    return (z * XS + x) * CORES + c


class Copies:
    def __init__(self, send, recv):
        self.send, self.recv, self.made = send, recv, []

    def start(self, src, dst, device):
        n = len(self.made)
        copy = pltpu.make_async_remote_copy(
            src_ref=src,
            dst_ref=dst,
            send_sem=self.send.at[n],
            recv_sem=self.recv.at[n],
            device_id=device,
            device_id_type=MESH,
        )
        copy.start()
        self.made.append(copy)
        return copy

    def finish(self):
        for copy in self.made:
            copy.wait_send()


def greet(devices):
    barrier = pltpu.get_barrier_semaphore()
    for device in devices:
        pl.semaphore_signal(barrier, inc=1, device_id=device, device_id_type=MESH)
    pl.semaphore_wait(barrier, len(devices))


def plane_offsets(inner_count):
    return [
        (dx, dc, di)
        for di in range(inner_count)
        for dx in range(XS)
        for dc in range(CORES)
        if (dx, dc, di) != (0, 0, 0)
    ]


def parts_of(value):
    high = value.astype(jnp.bfloat16)
    return high, (value - high.astype(jnp.float32)).astype(jnp.bfloat16)


def product(left, right, dims):
    def dot(a, b):
        return lax.dot_general(a, b, (dims, ((), ())), preferred_element_type=jnp.float32)

    total = dot(left[0], right[0])
    if len(right) > 1:
        total = total + dot(left[0], right[1])
    if len(left) > 1:
        total = total + dot(left[1], right[0])
    return total


PLAIN = ((1,), (0,))
LEFT_T = ((0,), (0,))
RIGHT_T = ((1,), (1,))


def step_kernel(
    zs, inner, cap, nb, rows, wide,
    owner_ref, g_ref, w_hbm, m1_hbm, m2_hbm, ls_hbm, rs_hbm, lb_hbm, rb_hbm,
    out_ref, m1_ref, m2_ref, ls_ref, rs_ref, lb_ref, rb_ref,
    block_ref, number_ref,
    w_in, m1_in, m2_in, ls_in, rs_in, lb_in, rb_in,
    b1, s1, r2a, s2a, f2a, r3a, r2b, s2b, f2b, r3b, total, zsend, zown, zrecv, psend, gbuf,
    grads, fresh, held,
    load, send, recv,
):
    z, x, c, i = position(inner)
    f32, bf16 = jnp.float32, jnp.bfloat16
    here = dp_of(z, x, c)
    core_peer = (dp_of(z, x, 1 - c), i)
    x_peer = (dp_of(z, 1 - x, c), i)

    def inner_peer(m):
        return (here, lax.rem(i + m, inner))

    def z_peer(k):
        return (dp_of(lax.rem(z + k, zs), x, c), i)

    def plane_peer(dx, dc, di):
        return (dp_of(z, lax.rem(x + dx, XS), lax.rem(c + dc, CORES)), lax.rem(i + di, inner))

    offsets = plane_offsets(inner)
    loads = []
    for n, (src, dst) in enumerate([
        (w_hbm, w_in), (m1_hbm, m1_in), (m2_hbm, m2_in), (ls_hbm, ls_in),
        (rs_hbm, rs_in), (lb_hbm, lb_in), (rb_hbm, rb_in),
    ]):
        loads.append(pltpu.make_async_copy(src, dst, load.at[n]))
    greet([plane_peer(*o) for o in offsets] + [z_peer(k) for k in range(1, zs)])

    copies = Copies(send, recv)
    half = nb // 2
    size = nb // PIECES
    pieces = []
    for p in range(PIECES // 2):
        pieces += [(True, p * size), (False, half + p * size)]

    first = [
        copies.start(g_ref.at[pl.ds(lo, size), 1 - c], b1.at[pl.ds(lo, size)], core_peer)
        for _, lo in pieces
    ]
    for copy in loads:
        copy.start()

    @pl.loop(0, zs * XS * CORES)
    def _(d):
        def look(b, state):
            seen, found = state
            hit = owner_ref[b] == d
            found = tuple(
                jnp.where(hit & (seen == n), b, old) for n, old in enumerate(found)
            )
            return seen + jnp.where(hit, 1, 0), found

        none = tuple(jnp.int32(-1) for _ in range(cap))
        _, found = lax.fori_loop(0, nb, look, (jnp.int32(0), none))
        for n in range(cap):
            block_ref[d * cap + n] = found[n]

    @pl.loop(0, nb)
    def _(b):
        def look(other, seen):
            return seen + jnp.where((owner_ref[other] == owner_ref[b]) & (other < b), 1, 0)

        number_ref[b] = lax.fori_loop(0, nb, look, jnp.int32(0))

    second = []
    for (inner_first, lo), arrived in zip(pieces, first):
        arrived.wait_recv()

        @pl.loop(lo, lo + size)
        def _(b):
            s1[b] = (g_ref[b, c].astype(f32) + b1[b].astype(f32)).astype(bf16)

        if inner_first:
            second.append([
                copies.start(
                    s1.at[pl.ds(lo, size), :, lax.rem(i + m, inner)],
                    r2a.at[m - 1, pl.ds(lo, size)],
                    inner_peer(m),
                )
                for m in range(1, inner)
            ])
        else:
            second.append([
                copies.start(
                    s1.at[pl.ds(lo, size), 1 - x], r2b.at[pl.ds(lo - half, size)], x_peer
                )
            ])
    third = []
    for (inner_first, lo), arrived in zip(pieces, second):
        for copy in arrived:
            copy.wait_recv()
        if inner_first:

            @pl.loop(lo, lo + size)
            def _(b):
                value = g_ref[b, c, :, i].astype(f32) + b1[b, :, i].astype(f32)
                for m in range(1, inner):
                    value = value + r2a[m - 1, b].astype(f32)
                f2a[b] = value
                s2a[b] = value.astype(bf16)

            third.append([
                copies.start(s2a.at[pl.ds(lo, size), 1 - x], r3a.at[pl.ds(lo, size)], x_peer)
            ])
        else:

            @pl.loop(lo, lo + size)
            def _(b):
                value = g_ref[b, c, x].astype(f32) + b1[b, x].astype(f32)
                value = value + r2b[b - half].astype(f32)
                f2b[b - half] = value
                s2b[b - half] = value.astype(bf16)

            third.append([
                copies.start(
                    s2b.at[pl.ds(lo - half, size), lax.rem(i + m, inner)],
                    r3b.at[m - 1, pl.ds(lo - half, size)],
                    inner_peer(m),
                )
                for m in range(1, inner)
            ])
    for (inner_first, lo), arrived in zip(pieces, third):
        for copy in arrived:
            copy.wait_recv()
        if inner_first:

            @pl.loop(lo, lo + size)
            def _(b):
                total[b] = f2a[b, x] + r3a[b].astype(f32)

        else:

            @pl.loop(lo, lo + size)
            def _(b):
                value = f2b[b - half, i]
                for m in range(1, inner):
                    value = value + r3b[m - 1, b - half].astype(f32)
                total[b] = value

    plane = XS * CORES * cap

    def slot_value(slot):
        block = block_ref[slot]
        value = total[jnp.maximum(block, 0)]
        return jnp.where(block >= 0, value, jnp.zeros_like(value))

    fourth = []
    for k in range(1, zs):
        there = lax.rem(z + k, zs)

        @pl.loop(0, plane)
        def _(s):
            zsend[k - 1, s] = slot_value(there * plane + s).astype(bf16)

        fourth.append(copies.start(zsend.at[k - 1], zrecv.at[k - 1], z_peer(k)))

    @pl.loop(0, plane)
    def _(s):
        zown[s] = slot_value(z * plane + s)

    for copy in fourth:
        copy.wait_recv()

    @pl.loop(0, plane)
    def _(s):
        value = zown[s]
        for k in range(1, zs):
            value = value + zrecv[k - 1, s].astype(f32)
        psend[s] = value.astype(bf16)

    share = (c * XS + x) * inner + i
    fifth = []
    for dx, dc, di in offsets:
        to = lax.rem(x + dx, XS) * CORES + lax.rem(c + dc, CORES)
        fifth.append(
            copies.start(
                psend.at[pl.ds(to * cap, cap)], gbuf.at[share], plane_peer(dx, dc, di)
            )
        )
    gbuf[share] = psend[pl.ds((x * CORES + c) * cap, cap)]
    for copy in fifth:
        copy.wait_recv()
    for s in range(CORES * XS * inner):
        grads[:, s * rows : (s + 1) * rows, :] = gbuf[s].astype(f32)
    for copy in loads:
        copy.wait()

    for k in range(cap):
        lb, rb = parts_of(lb_in[k]), parts_of(rb_in[k])
        half_turn = product(lb, (grads[k].astype(bf16),), LEFT_T)
        rotated = product(parts_of(half_turn), rb, PLAIN)
        first = SMOOTHING * m1_in[k] + (1.0 - SMOOTHING) * rotated
        second = SMOOTHING * m2_in[k] + (1.0 - SMOOTHING) * rotated * rotated
        m1_ref[k] = first
        m2_ref[k] = second
        direction = first / BIAS_CORRECTION / (jnp.sqrt(second / BIAS_CORRECTION) + 1e-08)
        back_turn = product(lb, parts_of(direction), PLAIN)
        update = product(parts_of(back_turn), rb, RIGHT_T)
        new = (w_in[k].astype(f32) - LEARNING_RATE * update).astype(bf16)
        for part in range(inner):
            for h in range(2):
                lo = (part * 2 + h) * wide
                fresh[part, h, k] = new[lo : lo + wide]

    def powers():
        @pl.loop(0, cap)
        def _(k):
            g = (grads[k].astype(bf16),)
            for in_ref, stats_ref, basis_in, basis_ref, dims in (
                (ls_in, ls_ref, lb_in, lb_ref, RIGHT_T),
                (rs_in, rs_ref, rb_in, rb_ref, LEFT_T),
            ):
                stats = SMOOTHING * in_ref[k] + (1.0 - SMOOTHING) * product(g, g, dims)
                stats_ref[k] = stats
                power = product(parts_of(stats), parts_of(basis_in[k]), PLAIN)
                norm = jnp.sqrt(jnp.sum(power * power, axis=(0, 1), keepdims=True))
                basis_ref[k] = power / (norm + 1e-06)

    def newton_schulz():
        @pl.loop(0, cap)
        def _(k):
            for basis_ref in (lb_ref, rb_ref):
                current = basis_ref[k]
                parts = parts_of(current)
                square = product(parts, parts, RIGHT_T)
                cubic = product(parts_of(square), parts, PLAIN)
                basis_ref[k] = 1.5 * current - 0.5 * cubic

    work = [powers] + [newton_schulz] * NS_STEPS
    mine_ref = fresh.at[i]
    own = held.at[z, x, i, c]
    along_z = [copies.start(mine_ref, own, z_peer(k)) for k in range(1, zs)]
    to_x, to_inner, to_core = [], [], []
    for k in range(zs):
        from_z = lax.rem(z + zs - k, zs)
        slot = held.at[from_z, x, i, c]
        if k > 0:
            along_z[k - 1].wait_recv()
        src = mine_ref if k == 0 else slot
        to_x.append(copies.start(src, slot, x_peer))
        to_inner.append([copies.start(src, slot, inner_peer(m)) for m in range(1, inner)])
        to_core.append(copies.start(src, slot, core_peer))
        if work:
            work.pop(0)()
    held[z, x, i, c] = fresh[i]
    corner = []
    for k in range(zs):
        from_z = lax.rem(z + zs - k, zs)
        slot = held.at[from_z, 1 - x, i, c]
        to_x[k].wait_recv()
        ahead = [
            copies.start(slot.at[0], slot.at[0], inner_peer(m)) for m in range(1, inner)
        ]
        to_core.append(copies.start(slot, slot, core_peer))
        for m in range(1, inner):
            from_i = lax.rem(i + inner - m, inner)
            slot = held.at[from_z, x, from_i, c]
            to_inner[k][m - 1].wait_recv()
            across = copies.start(slot.at[1], slot.at[1], x_peer)
            to_core.append(copies.start(slot, slot, core_peer))
            corner.append((from_z, from_i, ahead[m - 1], across))
        if work:
            work.pop(0)()
    for task in work:
        task()
    for from_z, from_i, ahead, across in corner:
        slot = held.at[from_z, 1 - x, from_i, c]
        ahead.wait_recv()
        to_core.append(copies.start(slot.at[0], slot.at[0], core_peer))
        across.wait_recv()
        to_core.append(copies.start(slot.at[1], slot.at[1], core_peer))
    for copy in to_core:
        copy.wait_recv()

    @pl.loop(0, nb)
    def _(b):
        d, bk = owner_ref[b], jnp.minimum(number_ref[b], cap - 1)
        bz, bx, bc = d // (XS * CORES), lax.rem(d // CORES, XS), lax.rem(d, CORES)
        for part in range(inner):
            for h in range(2):
                lo = (part * 2 + h) * wide
                out_ref[b, lo : lo + wide, :] = held[bz, bx, part, bc, h, bk]

    copies.finish()


def local(grad_parts, owner, *state):
    zs = lax.axis_size("dp") // (XS * CORES)
    inner = lax.axis_size("inner")
    nb, order = grad_parts.shape[1], grad_parts.shape[2]
    cap = state[0].shape[0]
    rows = order // (CORES * XS * inner)
    wide = order // (inner * 2)
    half = nb // 2
    plane = XS * CORES * cap
    f32, bf16 = jnp.float32, jnp.bfloat16
    tile = (rows, order)
    g = grad_parts.reshape(nb, CORES, XS, inner, rows, order)
    offsets = len(plane_offsets(inner))
    others = inner - 1
    count = PIECES + PIECES * inner + (zs - 1) + offsets
    count += (zs - 1) + zs * (2 + others) + zs * (1 + 3 * others) + zs * 2 * others
    smem = pl.BlockSpec(memory_space=pltpu.SMEM)
    vmem = pl.BlockSpec(memory_space=pltpu.VMEM)
    anywhere = pl.BlockSpec(memory_space=pl.ANY)
    square = jax.ShapeDtypeStruct((cap, order, order), f32)
    return pl.pallas_call(
        functools.partial(step_kernel, zs, inner, cap, nb, rows, wide),
        out_shape=(jax.ShapeDtypeStruct((nb, order, order), bf16),) + (square,) * 6,
        in_specs=[smem, vmem] + [anywhere] * 7,
        out_specs=(vmem,) * 7,
        scratch_shapes=[
            pltpu.SMEM((zs * plane,), jnp.int32),
            pltpu.SMEM((nb,), jnp.int32),
        ]
        + [pltpu.VMEM((cap, order, order), a.dtype) for a in state]
        + [
            pltpu.VMEM((nb, XS, inner) + tile, bf16),
            pltpu.VMEM((nb, XS, inner) + tile, bf16),
            pltpu.VMEM((inner - 1, half, XS) + tile, bf16),
            pltpu.VMEM((half, XS) + tile, bf16),
            pltpu.VMEM((half, XS) + tile, f32),
            pltpu.VMEM((half,) + tile, bf16),
            pltpu.VMEM((half, inner) + tile, bf16),
            pltpu.VMEM((half, inner) + tile, bf16),
            pltpu.VMEM((half, inner) + tile, f32),
            pltpu.VMEM((inner - 1, half) + tile, bf16),
            pltpu.VMEM((nb,) + tile, f32),
            pltpu.VMEM((zs - 1, plane) + tile, bf16),
            pltpu.VMEM((plane,) + tile, f32),
            pltpu.VMEM((zs - 1, plane) + tile, bf16),
            pltpu.VMEM((plane,) + tile, bf16),
            pltpu.VMEM((CORES * XS * inner, cap) + tile, bf16),
            pltpu.VMEM((cap, order, order), f32),
            pltpu.VMEM((inner, 2, cap, wide, order), bf16),
            pltpu.VMEM((zs, XS, inner, CORES, 2, cap, wide, order), bf16),
            pltpu.SemaphoreType.DMA((7,)),
            pltpu.SemaphoreType.DMA((count,)),
            pltpu.SemaphoreType.DMA((count,)),
        ],
        compiler_params=pltpu.CompilerParams(
            collective_id=0, has_side_effects=True, vmem_limit_bytes=60 * 1024 * 1024
        ),
    )(owner, g, *state)


def solution(mesh):
    dp = P("dp", None, None)
    in_specs = (P(("dp", "inner"), None, None, None), P()) + (dp,) * 7
    out_specs = (P(),) + (dp,) * 6
    return jax.shard_map(local, mesh=mesh, in_specs=in_specs, out_specs=out_specs, check_vma=False)
```

time: 93.6 us -> 82.5 us (0.88)
  matrix products: 15.6 us -> 0 us
  local copies, waits for them, and re-layouts: 2.99 us -> 8.37 us
  other arithmetic: 2.92 us -> 0 us
  Pallas kernels: 70.8 us -> 73.3 us
    dot_general x28 -> x0, matrix products: 15.6 us -> none  [the longest x10 5.93 us: orthonormalize(): jnp.einsum('cik,ckj->cij', square, current, precision=PRECISE)]
    unnamed x27 -> x19, local copies, waits for them, and re-layouts: 2.32 us -> 8.37 us
    pallas_call x2 -> x1, Pallas kernels: 70.8 us -> 73.3 us  [local(): pl.pallas_call(functools.partial(step_kernel, zs, inner, cap, nb, rows, w...]
    reduce_sum x2 -> x0, other arithmetic: 1.6 us -> none  [the longest x1 0.99 us: slot_numbers(): return jnp.sum(earlier.astype(jnp.int32), axis=1)]
where the time goes in v2:
time: 82.5 us; the launch traced here: 82.3 us
  Pallas kernels  73.3 us (89%)
  local copies, waits for them, and re-layouts  8.37 us (10%)
    pallas_call x1, Pallas kernels, local(): pl.pallas_call(functools.partial(step_kernel, zs, inner, cap, nb, rows, w...  73.3 us
    unnamed x19, local copies, waits for them, and re-layouts  8.37 us

profile of v2, /device:TPU:25, one launch (start us, length us, event | category | flops | bytes accessed | tf_op | source)
XLA Modules:
  0.0 82.3 jit_solution(7803349129915651829)
XLA Ops:
  0.6 73.3 %shard_map.144 = (bf16[20,256,256]{2,1,0:T(8,128)(2,1)}, f32[2,256,256]{2,1,0:T(8,128)}, f32[2,256,256]{2,1,0:T(8,128)}, f32[2,256,256]{2,1,0:T(8,128)}, f32[2,2...) custom-call(s32[20]{0:T(128)} %owner_ref.1, bf16[20,2,2,2,32,256]{5,4,3,2,1,0:T(8,128)(2,1)} %bitcast.1, ...), custom_call_target="tpu_custom_call" | custom-call | tf_op jit(solution)/shard_map/pallas_call | solution.py:409
  73.9 0.0 copy-start.5
  73.9 0.0 copy-start.4
  73.9 0.0 copy-start.3
  73.9 3.6 %copy.23 = bf16[20,256,256]{2,1,0:T(8,128)(2,1)} copy(bf16[20,256,256]{2,1,0:T(8,128)(2,1)} %get-tuple-element.14) | data formatting | bytes 5242880
  77.5 0.0 copy-done.5
  77.5 0.0 copy-start.2
  77.5 0.0 copy-start.1
  77.5 0.0 copy-start
  77.5 0.8 copy.24
  78.3 0.0 copy-done.4
  78.3 0.8 copy.25
  79.1 0.0 copy-done.3
  79.1 0.8 copy.26
  79.9 0.0 copy-done.2
  79.9 0.8 copy.27
  80.7 0.0 copy-done.1
  80.7 0.8 copy.28
  81.5 0.0 copy-done
  81.5 0.8 copy.29
Async XLA Ops:
  73.9 3.6 %copy-start.5 = (f32[2,256,256]{2,1,0:T(8,128)S(1)}, f32[2,256,256]{2,1,0:T(8,128)}, u32[]{:S(2)}) copy-start(f32[2,256,256]{2,1,0:T(8,128)} %get-tuple-element.15) | copy-start | bytes 1572868
  73.9 4.4 %copy-start.4 = (f32[2,256,256]{2,1,0:T(8,128)S(1)}, f32[2,256,256]{2,1,0:T(8,128)}, u32[]{:S(2)}) copy-start(f32[2,256,256]{2,1,0:T(8,128)} %get-tuple-element.16) | copy-start | bytes 1572868
  73.9 5.2 %copy-start.3 = (f32[2,256,256]{2,1,0:T(8,128)S(1)}, f32[2,256,256]{2,1,0:T(8,128)}, u32[]{:S(2)}) copy-start(f32[2,256,256]{2,1,0:T(8,128)} %get-tuple-element.17) | copy-start | bytes 1572868
  77.5 2.4 %copy-start.2 = (f32[2,256,256]{2,1,0:T(8,128)S(1)}, f32[2,256,256]{2,1,0:T(8,128)}, u32[]{:S(2)}) copy-start(f32[2,256,256]{2,1,0:T(8,128)} %get-tuple-element.18) | copy-start | bytes 1572868
  77.5 3.2 %copy-start.1 = (f32[2,256,256]{2,1,0:T(8,128)S(1)}, f32[2,256,256]{2,1,0:T(8,128)}, u32[]{:S(2)}) copy-start(f32[2,256,256]{2,1,0:T(8,128)} %get-tuple-element.19) | copy-start | bytes 1572868
  77.5 4.0 %copy-start = (f32[2,256,256]{2,1,0:T(8,128)S(1)}, f32[2,256,256]{2,1,0:T(8,128)}, u32[]{:S(2)}) copy-start(f32[2,256,256]{2,1,0:T(8,128)} %get-tuple-element.20) | copy-start | bytes 1572868

commit v3 on v2

--- a/solution.py
+++ b/solution.py
@@ -16,7 +16,7 @@
 MESH = pl.DeviceIdType.MESH
 CORES = 2
 XS = 2
-PIECES = 4
+PIECES = 10
 
 
 def position(inner_count):
@@ -96,9 +96,9 @@
 
 def step_kernel(
     zs, inner, cap, nb, rows, wide,
-    owner_ref, g_ref, w_hbm, m1_hbm, m2_hbm, ls_hbm, rs_hbm, lb_hbm, rb_hbm,
+    owner_ref, g_hbm, w_hbm, m1_hbm, m2_hbm, ls_hbm, rs_hbm, lb_hbm, rb_hbm,
     out_ref, m1_ref, m2_ref, ls_ref, rs_ref, lb_ref, rb_ref,
-    block_ref, number_ref,
+    block_ref, number_ref, g_ref,
     w_in, m1_in, m2_in, ls_in, rs_in, lb_in, rb_in,
     b1, s1, r2a, s2a, f2a, r3a, r2b, s2b, f2b, r3b, total, zsend, zown, zrecv, psend, gbuf,
     grads, fresh, held,
@@ -126,6 +126,8 @@
         (rs_hbm, rs_in), (lb_hbm, lb_in), (rb_hbm, rb_in),
     ]):
         loads.append(pltpu.make_async_copy(src, dst, load.at[n]))
+    own_grads = pltpu.make_async_copy(g_hbm.at[:, c], g_ref, load.at[7])
+    own_grads.start()
     greet([plane_peer(*o) for o in offsets] + [z_peer(k) for k in range(1, zs)])
 
     copies = Copies(send, recv)
@@ -136,7 +138,7 @@
         pieces += [(True, p * size), (False, half + p * size)]
 
     first = [
-        copies.start(g_ref.at[pl.ds(lo, size), 1 - c], b1.at[pl.ds(lo, size)], core_peer)
+        copies.start(g_hbm.at[pl.ds(lo, size), 1 - c], b1.at[pl.ds(lo, size)], core_peer)
         for _, lo in pieces
     ]
     for copy in loads:
@@ -164,13 +166,14 @@
 
         number_ref[b] = lax.fori_loop(0, nb, look, jnp.int32(0))
 
+    own_grads.wait()
     second = []
     for (inner_first, lo), arrived in zip(pieces, first):
         arrived.wait_recv()
 
         @pl.loop(lo, lo + size)
         def _(b):
-            s1[b] = (g_ref[b, c].astype(f32) + b1[b].astype(f32)).astype(bf16)
+            s1[b] = (g_ref[b].astype(f32) + b1[b].astype(f32)).astype(bf16)
 
         if inner_first:
             second.append([
@@ -195,7 +198,7 @@
 
             @pl.loop(lo, lo + size)
             def _(b):
-                value = g_ref[b, c, :, i].astype(f32) + b1[b, :, i].astype(f32)
+                value = g_ref[b, :, i].astype(f32) + b1[b, :, i].astype(f32)
                 for m in range(1, inner):
                     value = value + r2a[m - 1, b].astype(f32)
                 f2a[b] = value
@@ -208,7 +211,7 @@
 
             @pl.loop(lo, lo + size)
             def _(b):
-                value = g_ref[b, c, x].astype(f32) + b1[b, x].astype(f32)
+                value = g_ref[b, x].astype(f32) + b1[b, x].astype(f32)
                 value = value + r2b[b - half].astype(f32)
                 f2b[b - half] = value
                 s2b[b - half] = value.astype(bf16)
@@ -386,6 +389,15 @@
     copies.finish()
 
 
+def finish_kernel(*refs):
+    done = refs[14]
+    copies = [pltpu.make_async_copy(refs[n], refs[7 + n], done.at[n]) for n in range(7)]
+    for copy in copies:
+        copy.start()
+    for copy in copies:
+        copy.wait()
+
+
 def local(grad_parts, owner, *state):
     zs = lax.axis_size("dp") // (XS * CORES)
     inner = lax.axis_size("inner")
@@ -406,14 +418,16 @@
     vmem = pl.BlockSpec(memory_space=pltpu.VMEM)
     anywhere = pl.BlockSpec(memory_space=pl.ANY)
     square = jax.ShapeDtypeStruct((cap, order, order), f32)
-    return pl.pallas_call(
+    shapes = (jax.ShapeDtypeStruct((nb, order, order), bf16),) + (square,) * 6
+    results = pl.pallas_call(
         functools.partial(step_kernel, zs, inner, cap, nb, rows, wide),
-        out_shape=(jax.ShapeDtypeStruct((nb, order, order), bf16),) + (square,) * 6,
-        in_specs=[smem, vmem] + [anywhere] * 7,
+        out_shape=(pltpu.VMEM((nb, order, order), bf16),) + (pltpu.VMEM((cap, order, order), f32),) * 6,
+        in_specs=[smem] + [anywhere] * 8,
         out_specs=(vmem,) * 7,
         scratch_shapes=[
             pltpu.SMEM((zs * plane,), jnp.int32),
             pltpu.SMEM((nb,), jnp.int32),
+            pltpu.VMEM((nb, XS, inner) + tile, bf16),
         ]
         + [pltpu.VMEM((cap, order, order), a.dtype) for a in state]
         + [
@@ -436,14 +450,22 @@
             pltpu.VMEM((cap, order, order), f32),
             pltpu.VMEM((inner, 2, cap, wide, order), bf16),
             pltpu.VMEM((zs, XS, inner, CORES, 2, cap, wide, order), bf16),
-            pltpu.SemaphoreType.DMA((7,)),
+            pltpu.SemaphoreType.DMA((8,)),
             pltpu.SemaphoreType.DMA((count,)),
             pltpu.SemaphoreType.DMA((count,)),
         ],
         compiler_params=pltpu.CompilerParams(
-            collective_id=0, has_side_effects=True, vmem_limit_bytes=60 * 1024 * 1024
+            collective_id=0, has_side_effects=True, vmem_limit_bytes=58 * 1024 * 1024
         ),
     )(owner, g, *state)
+    return pl.pallas_call(
+        finish_kernel,
+        out_shape=shapes,
+        in_specs=[anywhere] * 7,
+        out_specs=(anywhere,) * 7,
+        scratch_shapes=[pltpu.SemaphoreType.DMA((7,))],
+        compiler_params=pltpu.CompilerParams(vmem_limit_bytes=1024 * 1024),
+    )(*results)
 
 
 def solution(mesh):

time: 82.5 us -> 73.8 us (0.89)
  local copies, waits for them, and re-layouts: 8.37 us -> 0 us
    unnamed x19 -> x0, local copies, waits for them, and re-layouts: 8.37 us -> none
    pallas_call x1, Pallas kernels: 73.3 us -> 70.5 us  [local(): pl.pallas_call(functools.partial(step_kernel, zs, inner, cap, nb, rows, w...]
    pallas_call x0 -> x1, Pallas kernels: none -> 2.55 us  [local(): pl.pallas_call(finish_kernel, out_shape=shapes, in_specs=[anywhere] * 7,...]
where the time goes in v3:
time: 73.8 us; the launch traced here: 73.7 us
  Pallas kernels  73 us (99%)
    pallas_call x1, Pallas kernels, local(): pl.pallas_call(functools.partial(step_kernel, zs, inner, cap, nb, rows, w...  70.5 us
    pallas_call x1, Pallas kernels, local(): pl.pallas_call(finish_kernel, out_shape=shapes, in_specs=[anywhere] * 7,...  2.55 us

profile of v3, /device:TPU:25, one launch (start us, length us, event | category | flops | bytes accessed | tf_op | source)
XLA Modules:
  0.0 73.7 jit_solution(8830686185653490721)
XLA Ops:
  0.6 70.5 %shard_map.144 = (bf16[20,256,256]{2,1,0:T(8,128)(2,1)S(1)}, f32[2,256,256]{2,1,0:T(8,128)S(1)}, f32[2,256,256]{2,1,0:T(8,128)S(1)}, f32[2,256,256]{2,1,0:T(8,12...) custom-call(s32[20]{0:T(128)} %owner_ref.1, ...), custom_call_target="tpu_custom_call" | custom-call | tf_op jit(solution)/shard_map/pallas_call | solution.py:422
  71.1 2.6 %shard_map.145 = (bf16[20,256,256]{2,1,0:T(8,128)(2,1)}, f32[2,256,256]{2,1,0:T(8,128)}, f32[2,256,256]{2,1,0:T(8,128)}, f32[2,256,256]{2,1,0:T(8,128)}, f32[2,2...) custom-call(bf16[20,256,256]{2,1,0:T(8,128)(2,1)S(1)} %get-tuple-element.14.refs_0_, ...), custom_call_target="tpu_custom_call" | custom-call | tf_op jit(solution)/shard_map/pallas_call | solution.py:461

commit v4 on v3

--- a/solution.py
+++ b/solution.py
@@ -335,21 +335,9 @@
     mine_ref = fresh.at[i]
     own = held.at[z, x, i, c]
     along_z = [copies.start(mine_ref, own, z_peer(k)) for k in range(1, zs)]
-    to_x, to_inner, to_core = [], [], []
-    for k in range(zs):
-        from_z = lax.rem(z + zs - k, zs)
-        slot = held.at[from_z, x, i, c]
-        if k > 0:
-            along_z[k - 1].wait_recv()
-        src = mine_ref if k == 0 else slot
-        to_x.append(copies.start(src, slot, x_peer))
-        to_inner.append([copies.start(src, slot, inner_peer(m)) for m in range(1, inner)])
-        to_core.append(copies.start(src, slot, core_peer))
-        if work:
-            work.pop(0)()
-    held[z, x, i, c] = fresh[i]
-    corner = []
-    for k in range(zs):
+    to_x, to_inner, to_core, corner = [], [], [], []
+
+    def forward(k):
         from_z = lax.rem(z + zs - k, zs)
         slot = held.at[from_z, 1 - x, i, c]
         to_x[k].wait_recv()
@@ -364,8 +352,24 @@
             across = copies.start(slot.at[1], slot.at[1], x_peer)
             to_core.append(copies.start(slot, slot, core_peer))
             corner.append((from_z, from_i, ahead[m - 1], across))
+
+    for k in range(zs):
+        from_z = lax.rem(z + zs - k, zs)
+        slot = held.at[from_z, x, i, c]
+        if k > 0:
+            along_z[k - 1].wait_recv()
+        src = mine_ref if k == 0 else slot
+        to_x.append(copies.start(src, slot, x_peer))
+        to_inner.append([copies.start(src, slot, inner_peer(m)) for m in range(1, inner)])
+        to_core.append(copies.start(src, slot, core_peer))
         if work:
             work.pop(0)()
+        if k > 0:
+            forward(k - 1)
+            if work:
+                work.pop(0)()
+    held[z, x, i, c] = fresh[i]
+    forward(zs - 1)
     for task in work:
         task()
     for from_z, from_i, ahead, across in corner:

time: 73.8 us -> 75.1 us (1.018)
  the two profiles are of different devices: /device:TPU:25 before, /device:TPU:17 now
where the time goes in v4:
time: 75.1 us; the launch traced here: 74.9 us
  Pallas kernels  74.3 us (99%)
    pallas_call x1, Pallas kernels, local(): pl.pallas_call(functools.partial(step_kernel, zs, inner, cap, nb, rows, w...  71.7 us
    pallas_call x1, Pallas kernels, local(): pl.pallas_call(finish_kernel, out_shape=shapes, in_specs=[anywhere] * 7,...  2.55 us

profile of v4, /device:TPU:17, one launch (start us, length us, event | category | flops | bytes accessed | tf_op | source)
XLA Modules:
  0.0 74.9 jit_solution(2820324140639366256)
XLA Ops:
  0.6 71.7 %shard_map.144 = (bf16[20,256,256]{2,1,0:T(8,128)(2,1)S(1)}, f32[2,256,256]{2,1,0:T(8,128)S(1)}, f32[2,256,256]{2,1,0:T(8,128)S(1)}, f32[2,256,256]{2,1,0:T(8,12...) custom-call(s32[20]{0:T(128)} %owner_ref.1, ...), custom_call_target="tpu_custom_call" | custom-call | tf_op jit(solution)/shard_map/pallas_call | solution.py:426
  72.4 2.6 %shard_map.145 = (bf16[20,256,256]{2,1,0:T(8,128)(2,1)}, f32[2,256,256]{2,1,0:T(8,128)}, f32[2,256,256]{2,1,0:T(8,128)}, f32[2,256,256]{2,1,0:T(8,128)}, f32[2,2...) custom-call(bf16[20,256,256]{2,1,0:T(8,128)(2,1)S(1)} %get-tuple-element.14.refs_0_, ...), custom_call_target="tpu_custom_call" | custom-call | tf_op jit(solution)/shard_map/pallas_call | solution.py:465
